TPU v7x, 256 devices: a whole 4x4x8 slice. The times are simulated.
256 devices in a mesh: dp: 8 (over y, core), expert: 32 (over z, x).
Axes of the slice: x: 4, y: 4, z: 8, core: 2. Of those that a mesh axis runs over, the one named last changes fastest.
Arguments:
- route_experts: int32 [32768, 8], P(('dp', 'expert')), may hold values from 0 to 255, all different within a row; in each aligned block of 128 rows (0 to 127, 128 to 255, ...) at most 5 rows name the same one
- router_gate_weight: float32 [32768, 8], P(('dp', 'expert')), may hold values from 0.02 to 0.3
- forget_mask: int32 [32768], P(('dp', 'expert')), may hold values 0 or 1
- retain_mask: int32 [32768], P(('dp', 'expert')), may hold values 0 or 1
- layer_output: bfloat16 [32768, 3584], P(('dp', 'expert')), may hold values from -6 to 6
- frozen_output: bfloat16 [32768, 3584], P(('dp', 'expert')), may hold values from -6 to 6
- control_vector: float32 [3584], replicated, may hold values from 0.1 to 1
- saved_hidden: bfloat16 [2048, 160, 2048], P(('dp', 'expert')), may hold values from -6 to 6
- adapter_in: bfloat16 [2048, 16384], P('dp', 'expert'), may hold values from -0.125 to 0.125
- adapter_out: bfloat16 [3584, 16384], P('dp', 'expert'), may hold values from -0.09375 to 0.09375
Outputs:
- grad_in: float32 [2048, 16384], P('dp', 'expert')
- grad_out: float32 [3584, 16384], P('dp', 'expert')
Inputs may be any that keep to these rules, and one draw needn't show every extreme that they name: `route_experts`: each row names 8 different experts; within the 128 rows of one device no expert is named more than 5 times, a bound that some block reaches.
All inputs are finite; a program needn't handle non-finite values. No bound on the sum of `forget_mask` or of `retain_mask` on one device may be relied on, other than what follows from the above.
Results may differ from a plain program's by a relative error of at most 0.0041.
Values may be sent and summed in bfloat16 or wider, within the bound.
No kernel may reach another device: no remote copies, remote signals or barrier semaphores. Data moves between devices by JAX's collectives and lax.ppermute only.
A program may use at most 128 MiB of HBM per device.

v0:
```python
import jax
import jax.numpy as jnp
from jax import lax
from jax.sharding import PartitionSpec as P

steer_coef = 20.0
retain_weight = 1.5
adapter_scale_factor = 2.0
grad_coef = 0.0625


def route_slots(experts_flat, count_all, capacity):
    onehot = (experts_flat[:, None] == jnp.arange(count_all, dtype=jnp.int32)[None, :]).astype(
        jnp.int32
    )
    running = jnp.cumsum(onehot, axis=0) - 1
    within = jnp.sum(onehot * running, axis=1)
    return experts_flat * capacity + within


def token_cotangent(layer_output, frozen_output, forget_mask, retain_mask, control_vector):
    unit = control_vector / jnp.sqrt(jnp.sum(control_vector * control_vector))
    current = layer_output.astype(jnp.float32)
    forget_term = current - steer_coef * unit[None, :]
    retain_term = current - frozen_output.astype(jnp.float32)
    forget_weight = forget_mask.astype(jnp.float32)[:, None]
    retain_part = retain_mask.astype(jnp.float32)[:, None]
    return grad_coef * (forget_weight * forget_term + retain_weight * retain_part * retain_term)


def local(
    route_experts,
    router_gate_weight,
    forget_mask,
    retain_mask,
    layer_output,
    frozen_output,
    control_vector,
    saved_hidden,
    adapter_in,
    adapter_out,
):
    experts_here = saved_hidden.shape[0]
    slot_count = saved_hidden.shape[1]
    hidden_width = saved_hidden.shape[2]
    feature_width = layer_output.shape[1]
    rank_width = adapter_in.shape[1] // experts_here
    expert_devices = lax.axis_size("expert")
    data_devices = lax.axis_size("dp")
    capacity = slot_count // expert_devices
    experts_all = experts_here * expert_devices
    output_gradient = token_cotangent(
        layer_output, frozen_output, forget_mask, retain_mask, control_vector
    )
    value_rows = (
        (router_gate_weight[:, :, None] * adapter_scale_factor * output_gradient[:, None, :])
        .reshape(-1, feature_width)
        .astype(jnp.bfloat16)
    )
    expert_slot_index = route_slots(route_experts.reshape(-1), experts_all, capacity)
    outgoing = (
        jnp.zeros((experts_all * capacity, feature_width), jnp.bfloat16)
        .at[expert_slot_index]
        .set(value_rows)
    )
    outgoing = outgoing.reshape(experts_all, capacity, feature_width)
    segment = lax.all_gather(adapter_in, "dp", axis=0, tiled=True)
    rows_now = segment.shape[0]
    hidden_part = saved_hidden
    factor = segment.reshape(rows_now, experts_here, rank_width)
    codes = jnp.einsum(
        "esf,fer->esr", hidden_part, factor, preferred_element_type=jnp.float32
    ).astype(jnp.bfloat16)
    arrived = lax.all_to_all(outgoing, "expert", split_axis=0, concat_axis=1, tiled=True)
    segment = lax.all_gather(adapter_out, "dp", axis=0, tiled=True)
    rows_now = segment.shape[0]
    arrived_part = arrived
    factor = segment.reshape(rows_now, experts_here, rank_width)
    back = jnp.einsum(
        "esd,der->esr", arrived_part, factor, preferred_element_type=jnp.float32
    ).astype(jnp.bfloat16)
    arrived_part = arrived
    product = jnp.einsum("esd,esr->der", arrived_part, codes, preferred_element_type=jnp.float32)
    grad_out = lax.psum_scatter(
        product.reshape(
            feature_width // data_devices * lax.axis_size("dp"), experts_here * rank_width
        ),
        "dp",
        scatter_dimension=0,
        tiled=True,
    )
    hidden_part = saved_hidden
    product = jnp.einsum("esf,esr->fer", hidden_part, back, preferred_element_type=jnp.float32)
    grad_in = lax.psum_scatter(
        product.reshape(
            hidden_width // data_devices * lax.axis_size("dp"), experts_here * rank_width
        ),
        "dp",
        scatter_dimension=0,
        tiled=True,
    )
    return (grad_in, grad_out)


def solution(mesh):
    return jax.shard_map(
        local,
        mesh=mesh,
        in_specs=(
            P(("dp", "expert"), None),
            P(("dp", "expert"), None),
            P(("dp", "expert")),
            P(("dp", "expert")),
            P(("dp", "expert"), None),
            P(("dp", "expert"), None),
            P(),
            P(("dp", "expert"), None, None),
            P("dp", "expert"),
            P("dp", "expert"),
        ),
        out_specs=(P("dp", "expert"), P("dp", "expert")),
        check_vma=False,
    )
```

profile of v0, /device:TPU:1, one launch (start us, length us, event | category | flops | bytes accessed | tf_op | source)
XLA Modules:
  0.0 537.4 jit_solution(12084886963748283533)
XLA Ops:
  7.2 0.0 copy-start.2
  7.2 0.0 copy-start.4
  7.2 0.0 copy-start.5
  7.2 0.0 copy-start.3
  7.2 0.0 copy-start
  7.2 0.9 copy.28
  8.1 0.1 eq.29
  8.2 0.1 eq.25
  8.3 0.7 broadcast_multiply_fusion.1
  9.0 0.1 copy.30
  9.1 0.2 fusion.21
  9.3 0.1 add_add_fusion
  9.4 0.3 copy.31
  9.7 0.1 copy.27
  9.8 0.1 mul.85
  9.9 0.0 copy-done.2
  10.0 0.6 multiply_reduce_fusion
  11.3 0.0 copy-done.4
  11.3 0.0 copy-done.5
  11.3 0.0 copy-done.3
  11.3 0.1 copy.32
  11.4 0.1 mul.89
  11.5 0.4 fusion.20
  11.9 0.0 copy-done
  11.9 1.7 fusion.12
  13.6 15.6 %scatter_custom_fusion = bf16[1280,3584]{1,0:T(8,128)(2,1)} fusion(s32[1024]{0:T(1024)S(1)} %bitcast.38, f32[128,3584]{1,0:T(8,128)S(1)} %fusion.12, f32[1024]{0:T(1024)S(1)} %mul.89, bf16[]{:T(256)} %constant.10.clone.1), kind=kCustom, calls=%fused_computation.7 | custom fusion | flops 7340032 | bytes 11014146 | tf_op jit(solution)/shard_map/scatter | solution.py:64
  29.2 14.6 %reshape.80 = bf16[256,5,3584]{2,1,0:T(8,128)(2,1)} reshape(bf16[1280,3584]{1,0:T(8,128)(2,1)} %scatter_custom_fusion) | data formatting | bytes 18350080 | tf_op jit(solution)/shard_map/reshape | solution.py:66
  43.8 0.0 copy-start.1
  43.8 12.1 %all-to-all-start = ((bf16[256,5,3584]{2,1,0:T(8,128)(2,1)}), bf16[256,5,3584]{2,1,0:T(8,128)(2,1)}, u32[]{:S(2)}, u32[]{:S(2)}) async-start(bf16[256,5,3584]{2,1,0:T(8,128)(2,1)} %reshape.80), calls=%async_computation | async-start | bytes 29360128 | tf_op jit(solution)/shard_map/all_to_all | solution.py:74
  55.9 0.0 all-gather.3.cloned.1.call-start
  56.0 0.7 all-gather.3.cloned.1.call-update
  56.6 0.0 all-gather.5.cloned.1.call-start
  56.7 0.0 copy-done.1
  56.7 0.8 copy.38
  57.5 0.0 all-gather.5.cloned.1.call-update
  57.6 0.0 reduce-scatter.3.cloned.1.call-start
  57.6 35.5 %all-gather.3.cloned.1.call-done = bf16[3584,512]{1,0:T(8,128)(2,1)} async-done(((bf16[448,512]{1,0:T(8,128)(2,1)}), bf16[3584,512]{1,0:T(8,128)(2,1)}) %all-gather.3.cloned.1.call-update) | async-done | bytes 3670032 | tf_op jit(solution)/shard_map/all_gather | solution.py:75
  93.1 5.9 %copy.35 = bf16[3584,512]{0,1:T(8,128)(2,1)} copy(bf16[3584,512]{1,0:T(8,128)(2,1)} %all-gather.3.cloned.1.call-done) | data formatting | bytes 7340032 | tf_op jit(solution)/shard_map/all_gather | solution.py:75
  99.0 296.3 %all-to-all-done = bf16[256,5,3584]{2,1,0:T(8,128)(2,1)} async-done(((bf16[256,5,3584]{2,1,0:T(8,128)(2,1)}), bf16[256,5,3584]{2,1,0:T(8,128)(2,1)}, u32[]{:S(2)}, u32[]{:S(2)}) %all-to-all-start) | async-done | bytes 9175072 | tf_op jit(solution)/shard_map/all_to_all | solution.py:74
  395.3 11.4 %copy.34 = bf16[8,32,5,3584]{3,0,2,1:T(8,128)(2,1)} copy(bf16[8,32,5,3584]{3,2,0,1:T(8,128)(2,1)} %bitcast.8) | data formatting | bytes 18350080 | tf_op jit(solution)/shard_map/all_to_all | solution.py:74
  406.7 12.2 %fusion.18 = f32[8,64,2048]{2,1,0:T(8,128)} fusion(bf16[8,160,2048]{2,1,0:T(8,128)(2,1)} %param.17, bf16[3584,8,64]{0,2,1:T(8,128)(2,1)} %bitcast.35, bf16[8,160,3584]{2,0,1:T(8,128)(2,1)} %bitcast.31), kind=kOutput, calls=%fused_computation.19 | convolution fusion | flops 922828800 | bytes 22282240 | tf_op jit(solution)/shard_map/esf,esr->fer/dot_general | solution.py:93
  418.8 5.3 copy.37
  424.2 0.0 reduce-scatter.3.cloned.1.call-update
  424.2 0.3 reduce-scatter.5.cloned.1.call-start
  424.5 0.0 all-gather.5.cloned.1.call-done
  424.5 16.2 %fusion.1 = f32[8,64,3584]{2,1,0:T(8,128)} fusion(bf16[8,160,3584]{2,0,1:T(8,128)(2,1)} %bitcast.32, bf16[8,160,2048]{2,1,0:T(8,128)(2,1)} %param.17, bf16[2048,8,64]{0,2,1:T(8,128)(2,1)} %bitcast.36), kind=kOutput, calls=%fused_computation.3 | convolution fusion | flops 922828800 | bytes 23855104 | tf_op jit(solution)/shard_map/esd,esr->der/dot_general | solution.py:83
  440.8 8.4 %copy.40 = f32[3584,512]{1,0:T(8,128)} copy(f32[3584,512]{0,1:T(8,128)} %bitcast.33) | data formatting | bytes 14680064 | tf_op jit(solution)/shard_map/reshape | solution.py:85
  449.1 0.0 reduce-scatter.5.cloned.1.call-update
  449.1 27.5 %reduce-scatter.3.cloned.1.call-done = f32[256,512]{1,0:T(8,128)} async-done(((f32[2048,512]{1,0:T(8,128)}), f32[256,512]{1,0:T(8,128)}) %reduce-scatter.3.cloned.1.call-update) | async-done | bytes 524304 | tf_op jit(solution)/shard_map/reduce_scatter | solution.py:94
  476.6 54.2 %reduce-scatter.5.cloned.1.call-done = f32[448,512]{1,0:T(8,128)} async-done(((f32[3584,512]{1,0:T(8,128)}), f32[448,512]{1,0:T(8,128)}) %reduce-scatter.5.cloned.1.call-update) | async-done | bytes 917520 | tf_op jit(solution)/shard_map/reduce_scatter | solution.py:84
  (8 shorter events, 0.1 us)
Async XLA Ops:
  7.2 2.8 copy-start.2
  7.2 4.1 copy-start.4
  7.2 4.1 copy-start.5
  7.2 4.1 copy-start.3
  7.2 4.7 copy-start
  43.8 12.9 %copy-start.1 = (bf16[256,512]{1,0:T(8,128)(2,1)S(1)}, bf16[256,512]{1,0:T(8,128)(2,1)}, u32[]{:S(2)}) copy-start(bf16[256,512]{1,0:T(8,128)(2,1)} %param.18) | copy-start | bytes 786436
  43.8 351.5 %all-to-all-start = ((bf16[256,5,3584]{2,1,0:T(8,128)(2,1)}), bf16[256,5,3584]{2,1,0:T(8,128)(2,1)}, u32[]{:S(2)}, u32[]{:S(2)}) async-start(bf16[256,5,3584]{2,1,0:T(8,128)(2,1)} %reshape.80), calls=%async_computation | async-start | bytes 29360128 | tf_op jit(solution)/shard_map/all_to_all | solution.py:74
  55.9 37.2 %all-gather.3.cloned.1.call-start = ((), (), s32[]{:S(2)}) async-start(), calls=%async_computation.3 | async-start | bytes 4128768 | tf_op jit(solution)/shard_map/all_gather | solution.py:75
  56.6 367.9 %all-gather.5.cloned.1.call-start = ((), (), s32[]{:S(2)}) async-start(), calls=%async_computation.5 | async-start | bytes 2359296 | tf_op jit(solution)/shard_map/all_gather | solution.py:67
  57.6 419.0 %reduce-scatter.3.cloned.1.call-start = ((), (), s32[]{:S(2)}) async-start(), calls=%async_computation.4 | async-start | bytes 4718592 | tf_op jit(solution)/shard_map/reduce_scatter | solution.py:94
  424.2 106.6 %reduce-scatter.5.cloned.1.call-start = ((), (), s32[]{:S(2)}) async-start(), calls=%async_computation.6 | async-start | bytes 8257536 | tf_op jit(solution)/shard_map/reduce_scatter | solution.py:84
Sparse Core Ops, SparseCore 0:
  58.6 34.4 all-gather.2
  95.5 29.2 all-gather.4
  424.3 52.2 reduce-scatter.2
  479.6 51.1 reduce-scatter.4
where the time goes:
time: 538 us; the launch traced here: 537 us
  waiting for transfers between devices  414 us (77%)
  local copies, waits for them, and re-layouts  48.3 us (9%)
  matrix products  28.4 us (5%)
  other arithmetic  19.3 us (4%)
  between operations  14.6 us (3%)
  starting transfers between devices  12.5 us (2%)
    all_to_all x1, waiting for transfers between devices, local(): lax.all_to_all(outgoing, 'expert', split_axis=0, concat_axis=1, tiled=True)  296 us
    reduce_scatter x1, waiting for transfers between devices, local(): lax.psum_scatter(product.reshape(feature_width // data_devices * lax.axis...  54.2 us
    all_gather x1, waiting for transfers between devices, local(): segment = lax.all_gather(adapter_out, 'dp', axis=0, tiled=True)  35.5 us
    reduce_scatter x1, waiting for transfers between devices, local(): lax.psum_scatter(product.reshape(hidden_width // data_devices * lax.axis_...  27.5 us
    dot_general x1, matrix products, local(): jnp.einsum('esd,esr->der', arrived_part, codes, preferred_element_type=jn...  16.2 us
    scatter x1, other arithmetic, local(): outgoing = jnp.zeros((experts_all * capacity, feature_width), jnp.bfloat1...  15.6 us
    reshape x1, local copies, waits for them, and re-layouts, local(): outgoing = outgoing.reshape(experts_all, capacity, feature_width)  14.6 us
    dot_general x1, matrix products, local(): jnp.einsum('esf,esr->fer', hidden_part, back, preferred_element_type=jnp....  12.2 us
  transfers between devices with their start and end apart: 5, of which 4 were waited for; matrix products, arithmetic and copies ran while one was open for 11% of the time, Pallas kernels for 0%

commit v1 on v0

--- a/solution.py
+++ b/solution.py
@@ -71,7 +71,9 @@
     codes = jnp.einsum(
         "esf,fer->esr", hidden_part, factor, preferred_element_type=jnp.float32
     ).astype(jnp.bfloat16)
-    arrived = lax.all_to_all(outgoing, "expert", split_axis=0, concat_axis=1, tiled=True)
+    pieces = jnp.split(outgoing, lax.axis_size("expert"), axis=0)
+    received = lax.all_to_all(jnp.stack(pieces), "expert", 0, 0)
+    arrived = jnp.concatenate(received, axis=1)
     segment = lax.all_gather(adapter_out, "dp", axis=0, tiled=True)
     rows_now = segment.shape[0]
     arrived_part = arrived

time: 538 us -> 483 us (0.90)
  waiting for transfers between devices: 414 us -> 277 us
  local copies, waits for them, and re-layouts: 48.3 us -> 126 us
    all_to_all x1, waiting for transfers between devices: 296 us -> 162 us  [local(): received = lax.all_to_all(jnp.stack(pieces), 'expert', 0, 0)]
    another operation x2 -> x36, local copies, waits for them, and re-layouts: 0.01 us -> 53.8 us  [the longest x34 53.8 us: local(): received = lax.all_to_all(jnp.stack(pieces), 'expert', 0, 0)]
    unnamed x14 -> x55, local copies, waits for them, and re-layouts: 1.74 us -> 43.3 us
    reshape x1 -> x0, local copies, waits for them, and re-layouts: 14.6 us -> none  [local(): outgoing = outgoing.reshape(experts_all, capacity, feature_width)]
    all_to_all x1 -> x0, local copies, waits for them, and re-layouts: 11.4 us -> none  [local(): lax.all_to_all(outgoing, 'expert', split_axis=0, concat_axis=1, tiled=True)]
    split x0 -> x2, local copies, waits for them, and re-layouts: none -> 8.02 us  [local(): pieces = jnp.split(outgoing, lax.axis_size('expert'), axis=0)]
  transfers between devices with their start and end apart: 5 -> 5, of which waited for: 4 -> 4; matrix products, arithmetic and copies ran while one was open for 11% -> 10% of each run, Pallas kernels for 0% -> 0%
where the time goes in v1:
time: 483 us; the launch traced here: 481 us
  waiting for transfers between devices  277 us (57%)
  local copies, waits for them, and re-layouts  126 us (26%)
  matrix products  28.5 us (6%)
  other arithmetic  23 us (5%)
  between operations  14.7 us (3%)
  starting transfers between devices  12.5 us (3%)
    all_to_all x1, waiting for transfers between devices, local(): received = lax.all_to_all(jnp.stack(pieces), 'expert', 0, 0)  162 us
    reduce_scatter x1, waiting for transfers between devices, local(): lax.psum_scatter(product.reshape(feature_width // data_devices * lax.axis...  54.2 us
    another operation x34, local copies, waits for them, and re-layouts, local(): received = lax.all_to_all(jnp.stack(pieces), 'expert', 0, 0)  53.8 us
    unnamed x55, local copies, waits for them, and re-layouts  43.3 us
    all_gather x1, waiting for transfers between devices, local(): segment = lax.all_gather(adapter_out, 'dp', axis=0, tiled=True)  35.2 us
    reduce_scatter x1, waiting for transfers between devices, local(): lax.psum_scatter(product.reshape(hidden_width // data_devices * lax.axis_...  24.3 us
    dot_general x1, matrix products, local(): jnp.einsum('esd,esr->der', arrived_part, codes, preferred_element_type=jn...  16.2 us
    scatter x1, other arithmetic, local(): outgoing = jnp.zeros((experts_all * capacity, feature_width), jnp.bfloat1...  15.7 us
  transfers between devices with their start and end apart: 5, of which 4 were waited for; matrix products, arithmetic and copies ran while one was open for 10% of the time, Pallas kernels for 0%

profile of v1, /device:TPU:1, one launch (start us, length us, event | category | flops | bytes accessed | tf_op | source)
XLA Modules:
  0.0 481.2 jit_solution(2297948641117503773)
XLA Ops:
  9.8 1.3 multiply_reduce_fusion
  15.1 2.0 fusion.12
  17.1 15.7 %scatter_custom_fusion = bf16[1280,3584]{1,0:T(8,128)(2,1)} fusion(s32[1024]{0:T(1024)S(1)} %bitcast.35, f32[128,3584]{1,0:T(8,128)S(1)} %fusion.12, f32[1024]{0:T(1024)S(1)} %mul.89, bf16[]{:T(256)} %constant.10.clone.1), kind=kCustom, calls=%fused_computation.7 | custom fusion | flops 7340032 | bytes 11014146 | tf_op jit(solution)/shard_map/scatter | solution.py:64
  32.8 3.1 fusion.25
  35.9 4.9 %fusion.24 = (bf16[40,3584]{1,0:T(8,128)(2,1)}, bf16[40,3584]{1,0:T(8,128)(2,1)}, bf16[40,3584]{1,0:T(8,128)(2,1)}, bf16[40,3584]{1,0:T(8,128)(2,1)}, bf16[40,35...) fusion(bf16[1280,3584]{1,0:T(8,128)(2,1)} %scatter_custom_fusion), kind=kLoop, calls=%fused_computation.67 | loop fusion | bytes 10895360 | tf_op jit(solution)/shard_map/split | solution.py:74
  40.8 1.1 stack.99
  42.7 1.9 stack.100
  44.5 1.8 stack.101
  46.4 0.9 stack.102
  47.3 0.9 stack.103
  48.2 0.9 stack.104
  49.1 0.9 stack.105
  50.0 0.9 stack.106
  50.9 0.9 stack.107
  51.8 0.9 stack.108
  52.7 0.9 stack.109
  53.6 0.9 stack.110
  54.5 0.9 stack.111
  55.4 1.8 stack.112
  57.2 1.9 stack.113
  59.1 1.8 stack.114
  60.9 1.9 stack.115
  62.8 1.8 stack.116
  64.6 1.8 stack.117
  66.4 1.8 stack.118
  68.3 1.9 stack.119
  70.1 1.9 stack.120
  72.0 1.9 stack.121
  73.9 1.9 stack.122
  75.7 1.9 stack.123
  77.6 1.1 stack.124
  78.7 1.1 stack.125
  79.7 1.1 stack.126
  80.8 1.1 stack.127
  82.0 1.1 stack.129
  83.3 2.0 constant_dynamic-update-slice_fusion.30
  85.3 1.8 constant_dynamic-update-slice_fusion.29
  87.2 1.8 constant_dynamic-update-slice_fusion.28
  89.0 1.9 constant_dynamic-update-slice_fusion.27
  90.8 1.8 constant_dynamic-update-slice_fusion.26
  92.7 1.8 constant_dynamic-update-slice_fusion.25
  94.5 1.8 constant_dynamic-update-slice_fusion.24
  96.3 1.8 constant_dynamic-update-slice_fusion.23
  98.1 1.8 constant_dynamic-update-slice_fusion.22
  99.9 1.8 constant_dynamic-update-slice_fusion.21
  101.7 1.8 constant_dynamic-update-slice_fusion.20
  103.6 1.8 constant_dynamic-update-slice_fusion.19
  105.4 1.8 constant_dynamic-update-slice_fusion.18
  107.2 1.8 constant_dynamic-update-slice_fusion.17
  109.1 1.8 constant_dynamic-update-slice_fusion.16
  110.9 1.8 constant_dynamic-update-slice_fusion.15
  113.5 0.9 constant_dynamic-update-slice_fusion.13
  114.4 0.9 constant_dynamic-update-slice_fusion.12
  125.0 11.4 %copy.32 = bf16[32,8,5,3584]{3,1,2,0:T(8,128)(2,1)} copy(bf16[32,8,5,3584]{3,2,1,0:T(8,128)(2,1)} %constant_dynamic-update-slice_fusion) | data formatting | bytes 18350080 | tf_op jit(solution)/shard_map/stack | solution.py:75
  136.4 12.1 %all-to-all-start = ((bf16[32,8,5,3584]{3,1,2,0:T(8,128)(2,1)}), bf16[32,8,5,3584]{3,1,2,0:T(8,128)(2,1)}, u32[]{:S(2)}, u32[]{:S(2)}) async-start(bf16[32,8,5,3584]{3,1,2,0:T(8,128)(2,1)} %copy.32), calls=%async_computation | async-start | bytes 18350080 | tf_op jit(solution)/shard_map/all_to_all | solution.py:75
  150.5 35.2 %all-gather.3.cloned.1.call-done = bf16[3584,512]{1,0:T(8,128)(2,1)} async-done(((bf16[448,512]{1,0:T(8,128)(2,1)}), bf16[3584,512]{1,0:T(8,128)(2,1)}) %all-gather.3.cloned.1.call-update) | async-done | bytes 3670032 | tf_op jit(solution)/shard_map/all_gather | solution.py:77
  185.7 5.9 %copy.33 = bf16[3584,512]{0,1:T(8,128)(2,1)} copy(bf16[3584,512]{1,0:T(8,128)(2,1)} %all-gather.3.cloned.1.call-done) | data formatting | bytes 7340032 | tf_op jit(solution)/shard_map/all_gather | solution.py:77
  191.6 162.1 %all-to-all-done = bf16[32,8,5,3584]{3,1,2,0:T(8,128)(2,1)} async-done(((bf16[32,8,5,3584]{3,1,2,0:T(8,128)(2,1)}), bf16[32,8,5,3584]{3,1,2,0:T(8,128)(2,1)}, u32[]{:S(2)}, u32[]{:S(2)}) %all-to-all-start) | async-done | bytes 9175072 | tf_op jit(solution)/shard_map/all_to_all | solution.py:75
  353.8 12.3 %fusion.18 = f32[8,64,2048]{2,1,0:T(8,128)} fusion(bf16[8,160,2048]{2,1,0:T(8,128)(2,1)} %param.17, bf16[3584,8,64]{0,2,1:T(8,128)(2,1)} %bitcast.32, bf16[8,160,3584]{2,0,1:T(8,128)(2,1)} %bitcast.7), kind=kOutput, calls=%fused_computation.19 | convolution fusion | flops 922828800 | bytes 22282240 | tf_op jit(solution)/shard_map/esf,esr->fer/dot_general | solution.py:95
  366.1 5.3 %copy.35 = f32[2048,512]{1,0:T(8,128)} copy(f32[2048,512]{0,1:T(8,128)} %bitcast.31) | data formatting | bytes 8388608 | tf_op jit(solution)/shard_map/reshape | solution.py:97
  371.5 16.2 %fusion.1 = f32[8,64,3584]{2,1,0:T(8,128)} fusion(bf16[8,160,3584]{2,0,1:T(8,128)(2,1)} %bitcast.7, bf16[8,160,2048]{2,1,0:T(8,128)(2,1)} %param.17, bf16[2048,8,64]{0,2,1:T(8,128)(2,1)} %bitcast.33), kind=kOutput, calls=%fused_computation.3 | convolution fusion | flops 922828800 | bytes 23855104 | tf_op jit(solution)/shard_map/esd,esr->der/dot_general | solution.py:85
  387.7 8.4 %copy.38 = f32[3584,512]{1,0:T(8,128)} copy(f32[3584,512]{0,1:T(8,128)} %bitcast.30) | data formatting | bytes 14680064 | tf_op jit(solution)/shard_map/reshape | solution.py:87
  396.1 24.3 %reduce-scatter.3.cloned.1.call-done = f32[256,512]{1,0:T(8,128)} async-done(((f32[2048,512]{1,0:T(8,128)}), f32[256,512]{1,0:T(8,128)}) %reduce-scatter.3.cloned.1.call-update) | async-done | bytes 524304 | tf_op jit(solution)/shard_map/reduce_scatter | solution.py:96
  420.5 54.2 %reduce-scatter.5.cloned.1.call-done = f32[448,512]{1,0:T(8,128)} async-done(((f32[3584,512]{1,0:T(8,128)}), f32[448,512]{1,0:T(8,128)}) %reduce-scatter.5.cloned.1.call-update) | async-done | bytes 917520 | tf_op jit(solution)/shard_map/reduce_scatter | solution.py:86
  (69 shorter events, 19.5 us)
Async XLA Ops:
  42.7 39.2 %copy-start.9 = (bf16[40,3584]{1,0:T(8,128)(2,1)S(1)}, bf16[40,3584]{1,0:T(8,128)(2,1)}, u32[]{:S(2)}) copy-start(bf16[40,3584]{1,0:T(8,128)(2,1)} %get-tuple-element.4) | copy-start | bytes 860164
  47.3 35.8 %copy-start.8 = (bf16[40,3584]{1,0:T(8,128)(2,1)S(1)}, bf16[40,3584]{1,0:T(8,128)(2,1)}, u32[]{:S(2)}) copy-start(bf16[40,3584]{1,0:T(8,128)(2,1)} %get-tuple-element.2) | copy-start | bytes 860164
  83.3 29.4 %copy-start.7 = (bf16[1,8,5,3584]{3,2,1,0:T(8,128)(2,1)S(1)}, bf16[1,8,5,3584]{3,2,1,0:T(8,128)(2,1)}, u32[]{:S(2)}) copy-start(bf16[1,8,5,3584]{3,2,1,0:T(8,128)(2,1)} %stack.116) | copy-start | bytes 860164
  83.3 30.2 %copy-start.6 = (bf16[1,8,5,3584]{3,2,1,0:T(8,128)(2,1)S(1)}, bf16[1,8,5,3584]{3,2,1,0:T(8,128)(2,1)}, u32[]{:S(2)}) copy-start(bf16[1,8,5,3584]{3,2,1,0:T(8,128)(2,1)} %stack.117) | copy-start | bytes 860164
  83.3 31.1 %copy-start.5 = (bf16[1,8,5,3584]{3,2,1,0:T(8,128)(2,1)S(1)}, bf16[1,8,5,3584]{3,2,1,0:T(8,128)(2,1)}, u32[]{:S(2)}) copy-start(bf16[1,8,5,3584]{3,2,1,0:T(8,128)(2,1)} %stack.118) | copy-start | bytes 860164
  83.3 32.0 %copy-start.4 = (bf16[1,8,5,3584]{3,2,1,0:T(8,128)(2,1)S(1)}, bf16[1,8,5,3584]{3,2,1,0:T(8,128)(2,1)}, u32[]{:S(2)}) copy-start(bf16[1,8,5,3584]{3,2,1,0:T(8,128)(2,1)} %stack.119) | copy-start | bytes 860164
  83.3 32.8 %copy-start.3 = (bf16[1,8,5,3584]{3,2,1,0:T(8,128)(2,1)S(1)}, bf16[1,8,5,3584]{3,2,1,0:T(8,128)(2,1)}, u32[]{:S(2)}) copy-start(bf16[1,8,5,3584]{3,2,1,0:T(8,128)(2,1)} %stack.120) | copy-start | bytes 860164
  83.3 33.6 %copy-start.2 = (bf16[1,8,5,3584]{3,2,1,0:T(8,128)(2,1)S(1)}, bf16[1,8,5,3584]{3,2,1,0:T(8,128)(2,1)}, u32[]{:S(2)}) copy-start(bf16[1,8,5,3584]{3,2,1,0:T(8,128)(2,1)} %stack.121) | copy-start | bytes 860164
  83.3 34.4 %copy-start.1 = (bf16[1,8,5,3584]{3,2,1,0:T(8,128)(2,1)S(1)}, bf16[1,8,5,3584]{3,2,1,0:T(8,128)(2,1)}, u32[]{:S(2)}) copy-start(bf16[1,8,5,3584]{3,2,1,0:T(8,128)(2,1)} %stack.122) | copy-start | bytes 860164
  83.3 35.2 %copy-start = (bf16[1,8,5,3584]{3,2,1,0:T(8,128)(2,1)S(1)}, bf16[1,8,5,3584]{3,2,1,0:T(8,128)(2,1)}, u32[]{:S(2)}) copy-start(bf16[1,8,5,3584]{3,2,1,0:T(8,128)(2,1)} %stack.123) | copy-start | bytes 860164
  136.4 12.9 %copy-start.10 = (bf16[256,512]{1,0:T(8,128)(2,1)S(1)}, bf16[256,512]{1,0:T(8,128)(2,1)}, u32[]{:S(2)}) copy-start(bf16[256,512]{1,0:T(8,128)(2,1)} %param.18) | copy-start | bytes 786436
  136.4 217.3 %all-to-all-start = ((bf16[32,8,5,3584]{3,1,2,0:T(8,128)(2,1)}), bf16[32,8,5,3584]{3,1,2,0:T(8,128)(2,1)}, u32[]{:S(2)}, u32[]{:S(2)}) async-start(bf16[32,8,5,3584]{3,1,2,0:T(8,128)(2,1)} %copy.32), calls=%async_computation | async-start | bytes 18350080 | tf_op jit(solution)/shard_map/all_to_all | solution.py:75
  148.5 37.2 %all-gather.3.cloned.1.call-start = ((), (), s32[]{:S(2)}) async-start(), calls=%async_computation.3 | async-start | bytes 4128768 | tf_op jit(solution)/shard_map/all_gather | solution.py:77
  149.3 222.2 %all-gather.5.cloned.1.call-start = ((), (), s32[]{:S(2)}) async-start(), calls=%async_computation.5 | async-start | bytes 2359296 | tf_op jit(solution)/shard_map/all_gather | solution.py:67
  150.2 270.3 %reduce-scatter.3.cloned.1.call-start = ((), (), s32[]{:S(2)}) async-start(), calls=%async_computation.4 | async-start | bytes 4718592 | tf_op jit(solution)/shard_map/reduce_scatter | solution.py:96
  371.4 103.2 %reduce-scatter.5.cloned.1.call-start = ((), (), s32[]{:S(2)}) async-start(), calls=%async_computation.6 | async-start | bytes 8257536 | tf_op jit(solution)/shard_map/reduce_scatter | solution.py:86
Sparse Core Ops, SparseCore 0:
  151.2 34.4 all-gather.2
  188.1 29.2 all-gather.4
  371.6 48.8 reduce-scatter.2
  423.5 51.1 reduce-scatter.4
